TPU v7x, 32 devices: a whole 2x2x4 slice. The times are simulated.
32 devices in a mesh: shot: 8 (over y, x, core), rcv: 4 (over z).
Axes of the slice: x: 2, y: 2, z: 4, core: 2. Of those that a mesh axis runs over, the one named last changes fastest.
Arguments:
- spectra: bfloat16 [4, 2, 2048, 2048], P(None, None, 'shot', 'rcv'), may hold values from -6 to 6
Outputs:
- multiples: float32 [4, 2, 2048, 2048], P('rcv', None, 'shot')
All inputs are finite; a program needn't handle non-finite values.
Results may differ from a plain program's by a relative error of at most 0.0003.
Values may be sent and summed in bfloat16 or wider, within the bound.
A program may use at most 128 MiB of HBM per device.

v0:
```python
import math
import jax
import jax.numpy as jnp
from jax import lax
from jax.sharding import PartitionSpec as P


def per_device(spectra):
    own_rows = lax.all_to_all(spectra, "rcv", split_axis=0, concat_axis=3, tiled=True)
    receiver_set_full = own_rows.shape[3]
    real_left_gathered = own_rows[:, 0]
    imaginary_left_gathered = own_rows[:, 1]
    shard_part = lax.all_gather(own_rows, "shot", axis=2, tiled=True)
    real_right_factor = shard_part[:, 0]
    imaginary_right_factor = shard_part[:, 1]
    real_out = jnp.einsum(
        "ang,agv->anv", real_left_gathered, real_right_factor, preferred_element_type=jnp.float32
    ) - jnp.einsum(
        "ang,agv->anv",
        imaginary_left_gathered,
        imaginary_right_factor,
        preferred_element_type=jnp.float32,
    )
    imag_out = jnp.einsum(
        "ang,agv->anv",
        real_left_gathered,
        imaginary_right_factor,
        preferred_element_type=jnp.float32,
    ) + jnp.einsum(
        "ang,agv->anv",
        imaginary_left_gathered,
        real_right_factor,
        preferred_element_type=jnp.float32,
    )
    result = jnp.stack([real_out, imag_out], axis=1)
    return result * (-1.0 / math.sqrt(receiver_set_full))


def solution(mesh):
    return jax.shard_map(
        per_device,
        mesh=mesh,
        in_specs=(P(None, None, "shot", "rcv"),),
        out_specs=P("rcv", None, "shot", None),
        check_vma=False,
    )
```

profile of v0, /device:TPU:0, one launch (start us, length us, event | category | flops | bytes accessed | tf_op | source)
XLA Modules:
  0.0 186.5 jit_solution(3624461053671120266)
XLA Ops:
  6.5 0.0 all-gather.2.cloned.1.call-start
  6.5 2.8 %copy.3 = bf16[4,2,256,512]{2,3,1,0:T(8,128)(2,1)S(1)} copy(bf16[4,2,256,512]{3,2,1,0:T(8,128)(2,1)} %param.1) | data formatting | bytes 4194304 | tf_op args[0]
  9.3 54.3 %all_to_all.18 = bf16[4,2,256,512]{2,3,1,0:T(8,128)(2,1)S(1)} all-to-all(bf16[4,2,256,512]{2,3,1,0:T(8,128)(2,1)S(1)} %copy.3), channel_id=1, replica_groups=mesh['shot'=8,'rcv'=4] {'rcv'}, dimensions={0} | all-to-all | bytes 4194304 | tf_op jit(solution)/shard_map/all_to_all | solution.py:9
  63.6 1.5 copy.4
  65.1 0.0 copy-start
  65.1 0.0 all-gather.2.cloned.1.call-update
  65.1 92.5 %all-gather.2.cloned.1.call-done = bf16[1,2,2048,2048]{2,3,1,0:T(8,128)(2,1)} async-done(((bf16[1,2,256,2048]{2,3,1,0:T(8,128)(2,1)}), bf16[1,2,2048,2048]{2,3,1,0:T(8,128)(2,1)}) %all-gather.2.cloned.1.call-update) | async-done | bytes 16777232 | tf_op jit(solution)/shard_map/all_gather | solution.py:13
  157.6 0.0 copy-done
  157.6 0.0 slice-start
  157.6 0.0 slice-start.1
  157.6 0.0 slice-start.2
  157.6 5.9 %fusion = f32[256,2048]{1,0:T(8,128)S(1)} fusion(bf16[1,2,2048,2048]{2,3,1,0:T(8,128)(2,1)} %all-gather.2.cloned.1.call-done, bf16[1,2,256,2048]{2,3,1,0:T(8,128)(2,1)S(1)} %bitcast.34), kind=kOutput, calls=%fused_computation.2 | convolution fusion | flops 2147483648 | bytes 11534336 | tf_op jit(solution)/shard_map/ang,agv->anv/dot_general | solution.py:29
  163.5 0.0 slice-start.3
  163.5 7.2 %fusion.1 = f32[256,2048]{1,0:T(8,128)} fusion(bf16[1,2,2048,2048]{2,3,1,0:T(8,128)(2,1)} %all-gather.2.cloned.1.call-done, bf16[1,2,256,2048]{2,3,1,0:T(8,128)(2,1)S(1)} %bitcast.35), kind=kOutput, calls=%fused_computation.3 | convolution fusion | flops 2147483648 | bytes 11534336 | tf_op jit(solution)/shard_map/ang,agv->anv/dot_general | solution.py:16
  170.8 0.0 slice-done
  170.8 0.0 slice-done.1
  170.8 0.0 slice-done.2
  170.8 0.0 slice-done.3
  170.8 2.4 %fusion.7 = f32[1,1,256,2048]{3,2,1,0:T(8,128)S(1)} fusion(f32[256,2048]{1,0:T(8,128)S(1)} %fusion, bf16[1,2,2048,2048]{2,3,1,0:T(8,128)(2,1)S(1)} %bitcast.39, bf16[1,2,256,2048]{2,3,1,0:T(8,128)(2,1)S(1)} %bitcast.36), kind=kOutput, calls=%fused_computation.10 | convolution fusion | flops 2148007936 | bytes 13631488 | tf_op jit(solution)/shard_map/ang,agv->anv/dot_general | solution.py:24
  173.2 4.0 %fusion.5 = f32[1,1,256,2048]{3,2,1,0:T(8,128)S(1)} fusion(f32[256,2048]{1,0:T(8,128)} %fusion.1, bf16[1,2,2048,2048]{2,3,1,0:T(8,128)(2,1)S(1)} %bitcast.39, bf16[1,2,256,2048]{2,3,1,0:T(8,128)(2,1)S(1)} %bitcast.37), kind=kOutput, calls=%fused_computation.8 | convolution fusion | flops 2148007936 | bytes 13631488 | tf_op jit(solution)/shard_map/ang,agv->anv/dot_general | solution.py:18
  177.2 2.4 %maximum_multiply_fusion = f32[1,2,256,2048]{3,2,1,0:T(8,128)} fusion(f32[1,1,256,2048]{3,2,1,0:T(8,128)S(1)} %fusion.7, f32[1,1,256,2048]{3,2,1,0:T(8,128)S(1)} %fusion.5), kind=kLoop, calls=%fused_computation.6 | loop fusion | flops 2097152 | bytes 8388608 | tf_op jit(solution)/shard_map/mul | solution.py:36
  (1 shorter events, 0.0 us)
Async XLA Ops:
  6.5 151.1 %all-gather.2.cloned.1.call-start = ((), (), s32[]{:S(2)}) async-start(), calls=%async_computation.1 | async-start | bytes 18874368 | tf_op jit(solution)/shard_map/all_gather | solution.py:13
  65.1 92.5 %copy-start = (bf16[4,2,256,512]{2,3,0,1:T(8,128)(2,1)S(1)}, bf16[4,2,256,512]{2,3,0,1:T(8,128)(2,1)}, u32[]{:S(2)}) copy-start(bf16[4,2,256,512]{2,3,0,1:T(8,128)(2,1)} %copy.4) | copy-start | bytes 6291460
  157.6 13.2 %slice-start = ((s8[16777216]{0:T(1024)(128)(4,1)}), s8[4194304]{0:T(1024)(128)(4,1)S(1)}, s32[]{:S(2)}) async-start(s8[16777216]{0:T(1024)(128)(4,1)} %bitcast.38), calls=%async_computation.2 | async-start | bytes 8388608
  157.6 13.2 %slice-start.1 = ((s8[16777216]{0:T(1024)(128)(4,1)}), s8[4194304]{0:T(1024)(128)(4,1)S(1)}, s32[]{:S(2)}) async-start(s8[16777216]{0:T(1024)(128)(4,1)} %bitcast.38), calls=%async_computation.3 | async-start | bytes 8388608
  157.6 13.2 %slice-start.2 = ((s8[16777216]{0:T(1024)(128)(4,1)}), s8[4194304]{0:T(1024)(128)(4,1)S(1)}, s32[]{:S(2)}) async-start(s8[16777216]{0:T(1024)(128)(4,1)} %bitcast.38), calls=%async_computation.4 | async-start | bytes 8388608
  163.5 7.3 %slice-start.3 = ((s8[16777216]{0:T(1024)(128)(4,1)}), s8[4194304]{0:T(1024)(128)(4,1)S(1)}, s32[]{:S(2)}) async-start(s8[16777216]{0:T(1024)(128)(4,1)} %bitcast.38), calls=%async_computation.5 | async-start | bytes 8388608
Sparse Core Ops, SparseCore 0:
  65.2 92.3 all-gather.1
where the time goes:
time: 187 us; the launch traced here: 186 us
  waiting for transfers between devices  92.5 us (49%)
  blocking collectives  54.3 us (29%)
  matrix products  19.5 us (10%)
  between operations  13.5 us (7%)
  local copies, waits for them, and re-layouts  4.23 us (2%)
  other arithmetic  2.43 us (1%)
    all_gather x1, waiting for transfers between devices, per_device(): shard_part = lax.all_gather(own_rows, 'shot', axis=2, tiled=True)  92.5 us
    all_to_all x1, blocking collectives, per_device(): lax.all_to_all(spectra, 'rcv', split_axis=0, concat_axis=3, tiled=True)  54.3 us
    dot_general x1, matrix products, per_device(): jnp.einsum('ang,agv->anv', real_left_gathered, real_right_factor, preferr...  7.24 us
    dot_general x1, matrix products, per_device(): jnp.einsum('ang,agv->anv', imaginary_left_gathered, real_right_factor, pr...  5.92 us
    dot_general x1, matrix products, per_device(): jnp.einsum('ang,agv->anv', imaginary_left_gathered, imaginary_right_facto...  3.98 us
  transfers between devices with their start and end apart: 1, of which 1 were waited for; matrix products, arithmetic and copies ran while one was open for 0% of the time, Pallas kernels for 0%

commit v1 on v0

--- a/solution.py
+++ b/solution.py
@@ -5,12 +5,28 @@
 from jax.sharding import PartitionSpec as P
 
 
+def ring_gather(x, axis, dim):
+    ways, here, lap = (lax.axis_size(axis), lax.axis_index(axis), x.shape[dim])
+    lengths = [n * ways if d == dim else n for d, n in enumerate(x.shape)]
+    full = lax.dynamic_update_slice_in_dim(jnp.zeros(lengths, x.dtype), x, here * lap, axis=dim)
+    going_up = going_down = x
+    for far in range(1, ways // 2 + 1):
+        going_up = lax.ppermute(going_up, axis, [(d, (d + 1) % ways) for d in range(ways)])
+        full = lax.dynamic_update_slice_in_dim(full, going_up, (here - far) % ways * lap, axis=dim)
+        if 2 * far < ways:
+            going_down = lax.ppermute(going_down, axis, [(d, (d - 1) % ways) for d in range(ways)])
+            full = lax.dynamic_update_slice_in_dim(
+                full, going_down, (here + far) % ways * lap, axis=dim
+            )
+    return full
+
+
 def per_device(spectra):
     own_rows = lax.all_to_all(spectra, "rcv", split_axis=0, concat_axis=3, tiled=True)
     receiver_set_full = own_rows.shape[3]
     real_left_gathered = own_rows[:, 0]
     imaginary_left_gathered = own_rows[:, 1]
-    shard_part = lax.all_gather(own_rows, "shot", axis=2, tiled=True)
+    shard_part = ring_gather(own_rows, "shot", 2)
     real_right_factor = shard_part[:, 0]
     imaginary_right_factor = shard_part[:, 1]
     real_out = jnp.einsum(

time: 187 us -> 248 us (1.33)
  waiting for transfers between devices: 92.5 us -> 149 us
  local copies, waits for them, and re-layouts: 4.23 us -> 24.4 us
  between operations: 13.5 us -> 0.17 us
  matrix products: 19.5 us -> 10 us
  starting transfers between devices: 0.01 us -> 5.49 us
    ppermute x0 -> x7, waiting for transfers between devices: none -> 149 us  [the longest x4 149 us: ring_gather(): lax.ppermute(going_up, axis, [(d, (d + 1) % ways) for d in range(ways)])]
    all_gather x1 -> x0, waiting for transfers between devices: 92.5 us -> none  [per_device(): shard_part = lax.all_gather(own_rows, 'shot', axis=2, tiled=True)]
    dynamic_update_slice x0 -> x8, local copies, waits for them, and re-layouts: none -> 9.23 us  [the longest x4 4.61 us: ring_gather(): lax.dynamic_update_slice_in_dim(full, going_up, (here - far) % ways * lap...]
    ppermute x0 -> x7, starting transfers between devices: none -> 5.49 us  [the longest x3 5.43 us: ring_gather(): lax.ppermute(going_down, axis, [(d, (d - 1) % ways) for d in range(ways)])]
    mul x0 -> x1, local copies, waits for them, and re-layouts: none -> 5.34 us  [per_device(): return result * (-1.0 / math.sqrt(receiver_set_full))]
    unnamed x11 -> x13, local copies, waits for them, and re-layouts: 2.78 us -> 7.65 us
    dot_general x1, matrix products: 7.24 us -> 2.52 us  [per_device(): jnp.einsum('ang,agv->anv', real_left_gathered, real_right_factor, preferr...]
    dot_general x1, matrix products: 5.92 us -> 2.48 us  [per_device(): jnp.einsum('ang,agv->anv', imaginary_left_gathered, real_right_factor, pr...]
  transfers between devices with their start and end apart: 1 -> 7, of which waited for: 1 -> 4; matrix products, arithmetic and copies ran while one was open for 0% -> 4% of each run, Pallas kernels for 0% -> 0%
where the time goes in v1:
time: 248 us; the launch traced here: 246 us
  waiting for transfers between devices  149 us (60%)
  blocking collectives  54.3 us (22%)
  local copies, waits for them, and re-layouts  24.4 us (10%)
  matrix products  10 us (4%)
  starting transfers between devices  5.49 us (2%)
    ppermute x4, waiting for transfers between devices, ring_gather(): lax.ppermute(going_up, axis, [(d, (d + 1) % ways) for d in range(ways)])  149 us
    all_to_all x1, blocking collectives, per_device(): lax.all_to_all(spectra, 'rcv', split_axis=0, concat_axis=3, tiled=True)  54.3 us
    unnamed x13, local copies, waits for them, and re-layouts  7.65 us
    ppermute x3, starting transfers between devices, ring_gather(): lax.ppermute(going_down, axis, [(d, (d - 1) % ways) for d in range(ways)])  5.43 us
    mul x1, local copies, waits for them, and re-layouts, per_device(): return result * (-1.0 / math.sqrt(receiver_set_full))  5.34 us
  transfers between devices with their start and end apart: 7, of which 4 were waited for; matrix products, arithmetic and copies ran while one was open for 4% of the time, Pallas kernels for 0%

profile of v1, /device:TPU:0, one launch (start us, length us, event | category | flops | bytes accessed | tf_op | source)
XLA Modules:
  0.0 246.0 jit_solution(545011859363614596)
XLA Ops:
  0.0 2.8 %copy.5 = bf16[4,2,256,512]{2,3,1,0:T(8,128)(2,1)S(1)} copy(bf16[4,2,256,512]{3,2,1,0:T(8,128)(2,1)} %param.1) | data formatting | bytes 4194304 | tf_op args[0]
  2.8 54.3 %all_to_all.18 = bf16[4,2,256,512]{2,3,1,0:T(8,128)(2,1)S(1)} all-to-all(bf16[4,2,256,512]{2,3,1,0:T(8,128)(2,1)S(1)} %copy.5), channel_id=1, replica_groups=mesh['shot'=8,'rcv'=4] {'rcv'}, dimensions={0} | all-to-all | bytes 4194304 | tf_op jit(solution)/shard_map/all_to_all | solution.py:25
  57.3 2.6 %collective-permute-start.1 = (bf16[1,2,256,2048]{2,3,1,0:T(8,128)(2,1)S(1)}, bf16[1,2,256,2048]{2,3,1,0:T(8,128)(2,1)S(1)}, u32[]{:S(2)}, u32[]{:S(2)}) collective-permute-start(bf16[1,2,256,2048]{2,3,1,0:T(8,128)(2,1)S(1)} %bitcast.38), channel_id=1, source_target_pairs={{0,28},{4,0},{8,4},{12,8},{16,12},{20,16},{24,20},{28,24},{1,29},{... | collective-permute-start | bytes 6291464 | tf_op jit(solution)/shard_map/ppermute | solution.py:17
  59.9 44.3 %collective-permute-done = bf16[1,2,256,2048]{2,3,1,0:T(8,128)(2,1)S(1)} collective-permute-done((bf16[1,2,256,2048]{2,3,1,0:T(8,128)(2,1)S(1)}, bf16[1,2,256,2048]{2,3,1,0:T(8,128)(2,1)S(1)}, u32[]{:S(2)}, u32[]{:S(2)}) %collective-permute-start) | collective-permute-done | bytes 2097184 | tf_op jit(solution)/shard_map/ppermute | solution.py:14
  104.2 1.3 copy-done
  105.5 1.5 collective-permute-start.3
  107.0 44.7 %collective-permute-done.2 = bf16[1,2,256,2048]{2,3,1,0:T(8,128)(2,1)S(1)} collective-permute-done((bf16[1,2,256,2048]{2,3,1,0:T(8,128)(2,1)S(1)}, bf16[1,2,256,2048]{2,3,1,0:T(8,128)(2,1)S(1)}, u32[]{:S(2)}, u32[]{:S(2)}) %collective-permute-start.2) | collective-permute-done | bytes 2097184 | tf_op jit(solution)/shard_map/ppermute | solution.py:14
  151.7 1.3 copy-done.4
  153.0 1.3 collective-permute-start.5
  154.3 45.3 %collective-permute-done.4 = bf16[1,2,256,2048]{2,3,1,0:T(8,128)(2,1)} collective-permute-done((bf16[1,2,256,2048]{2,3,1,0:T(8,128)(2,1)S(1)}, bf16[1,2,256,2048]{2,3,1,0:T(8,128)(2,1)}, u32[]{:S(2)}, u32[]{:S(2)}) %collective-permute-start.4) | collective-permute-done | bytes 2097184 | tf_op jit(solution)/shard_map/ppermute | solution.py:14
  199.7 2.0 broadcast_in_dim.3
  202.1 1.2 copy-done.1
  204.3 0.8 copy-done.5
  205.4 2.0 constant_dynamic-update-slice_fusion.3
  207.4 1.9 constant_dynamic-update-slice_fusion.2
  209.4 2.0 constant_dynamic-update-slice_fusion.1
  211.3 15.0 %collective-permute-done.6 = bf16[1,2,256,2048]{2,3,1,0:T(8,128)(2,1)} collective-permute-done((bf16[1,2,256,2048]{2,3,1,0:T(8,128)(2,1)}, bf16[1,2,256,2048]{2,3,1,0:T(8,128)(2,1)}, u32[]{:S(2)}, u32[]{:S(2)}) %collective-permute-start.6) | collective-permute-done | bytes 2097184 | tf_op jit(solution)/shard_map/ppermute | solution.py:14
  226.3 1.9 constant_dynamic-update-slice_fusion
  228.3 2.5 %fusion.3 = f32[2048,256]{1,0:T(8,128)S(1)} fusion(bf16[1,2,2048,2048]{2,3,1,0:T(8,128)(2,1)S(1)} %constant_dynamic-update-slice_fusion, bf16[1,2,256,2048]{2,3,1,0:T(8,128)(2,1)S(1)} %bitcast.40), kind=kOutput, calls=%fused_computation.5 | convolution fusion | flops 2147483648 | bytes 11534336 | tf_op jit(solution)/shard_map/ang,agv->anv/dot_general | solution.py:34
  230.8 2.5 %fusion = f32[2048,256]{1,0:T(8,128)S(1)} fusion(bf16[1,2,2048,2048]{2,3,1,0:T(8,128)(2,1)S(1)} %constant_dynamic-update-slice_fusion, bf16[1,2,256,2048]{2,3,1,0:T(8,128)(2,1)S(1)} %bitcast.41), kind=kOutput, calls=%fused_computation.2 | convolution fusion | flops 2147483648 | bytes 11534336 | tf_op jit(solution)/shard_map/ang,agv->anv/dot_general | solution.py:45
  233.3 2.5 %fusion.7 = f32[1,1,256,2048]{2,3,1,0:T(8,128)S(1)} fusion(f32[2048,256]{1,0:T(8,128)S(1)} %fusion.3, bf16[1,2,2048,2048]{2,3,1,0:T(8,128)(2,1)S(1)} %constant_dynamic-update-slice_fusion, bf16[1,2,256,2048]{2,3,1,0:T(8,128)(2,1)S(1)} %bitcast.42), kind=kOutput, calls=%fused_computation.10 | convolution fusion | flops 2148007936 | bytes 13631488 | tf_op jit(solution)/shard_map/ang,agv->anv/dot_general | solution.py:32
  235.8 2.5 %fusion.5 = f32[1,1,256,2048]{2,3,1,0:T(8,128)S(1)} fusion(f32[2048,256]{1,0:T(8,128)S(1)} %fusion, bf16[1,2,2048,2048]{2,3,1,0:T(8,128)(2,1)S(1)} %constant_dynamic-update-slice_fusion, bf16[1,2,256,2048]{2,3,1,0:T(8,128)(2,1)S(1)} %bitcast.43), kind=kOutput, calls=%fused_computation.8 | convolution fusion | flops 2148007936 | bytes 13631488 | tf_op jit(solution)/shard_map/ang,agv->anv/dot_general | solution.py:40
  238.3 2.3 maximum_multiply_fusion
  240.7 5.3 %copy.7 = f32[1,2,256,2048]{3,2,1,0:T(8,128)} copy(f32[1,2,256,2048]{2,3,1,0:T(8,128)} %maximum_multiply_fusion) | data formatting | bytes 8388608 | tf_op jit(solution)/shard_map/mul | solution.py:52
  (20 shorter events, 1.9 us)
Async XLA Ops:
  57.2 47.0 %collective-permute-start = (bf16[1,2,256,2048]{2,3,1,0:T(8,128)(2,1)S(1)}, bf16[1,2,256,2048]{2,3,1,0:T(8,128)(2,1)S(1)}, u32[]{:S(2)}, u32[]{:S(2)}) collective-permute-start(bf16[1,2,256,2048]{2,3,1,0:T(8,128)(2,1)S(1)} %bitcast.37), channel_id=1, source_target_pairs={{0,4},{4,8},{8,12},{12,16},{16,20},{20,24},{24,28},{28,0},{1,5},{5... | collective-permute-start | bytes 6291464 | tf_op jit(solution)/shard_map/ppermute | solution.py:14
  57.3 46.9 %collective-permute-start.1 = (bf16[1,2,256,2048]{2,3,1,0:T(8,128)(2,1)S(1)}, bf16[1,2,256,2048]{2,3,1,0:T(8,128)(2,1)S(1)}, u32[]{:S(2)}, u32[]{:S(2)}) collective-permute-start(bf16[1,2,256,2048]{2,3,1,0:T(8,128)(2,1)S(1)} %bitcast.38), channel_id=1, source_target_pairs={{0,28},{4,0},{8,4},{12,8},{16,12},{20,16},{24,20},{28,24},{1,29},{... | collective-permute-start | bytes 6291464 | tf_op jit(solution)/shard_map/ppermute | solution.py:17
  104.2 1.3 copy-start
  104.2 47.5 %collective-permute-start.2 = (bf16[1,2,256,2048]{2,3,1,0:T(8,128)(2,1)S(1)}, bf16[1,2,256,2048]{2,3,1,0:T(8,128)(2,1)S(1)}, u32[]{:S(2)}, u32[]{:S(2)}) collective-permute-start(bf16[1,2,256,2048]{2,3,1,0:T(8,128)(2,1)S(1)} %collective-permute-done), channel_id=1, source_target_pairs={{0,4},{4,8},{8,12},{12,16},{16,20},{20,24},{24,28},{28,0},{1,5},{5... | collective-permute-start | bytes 6291464 | tf_op jit(solution)/shard_map/ppermute | solution.py:14
  105.5 46.2 %copy-start.2 = (bf16[1,2,256,2048]{2,3,1,0:T(8,128)(2,1)}, bf16[1,2,256,2048]{2,3,1,0:T(8,128)(2,1)S(1)}, u32[]{:S(2)}) copy-start(bf16[1,2,256,2048]{2,3,1,0:T(8,128)(2,1)S(1)} %collective-permute-done.1) | copy-start | bytes 6291460
  105.5 46.2 %collective-permute-start.3 = (bf16[1,2,256,2048]{2,3,1,0:T(8,128)(2,1)S(1)}, bf16[1,2,256,2048]{2,3,1,0:T(8,128)(2,1)}, u32[]{:S(2)}, u32[]{:S(2)}) collective-permute-start(bf16[1,2,256,2048]{2,3,1,0:T(8,128)(2,1)S(1)} %collective-permute-done.1), channel_id=1, source_target_pairs={{0,28},{4,0},{8,4},{12,8},{16,12},{20,16},{24,20},{28,24},{1,29},{... | collective-permute-start | bytes 6291464 | tf_op jit(solution)/shard_map/ppermute | solution.py:17
  151.7 1.4 copy-start.4
  151.7 48.0 %collective-permute-start.4 = (bf16[1,2,256,2048]{2,3,1,0:T(8,128)(2,1)S(1)}, bf16[1,2,256,2048]{2,3,1,0:T(8,128)(2,1)}, u32[]{:S(2)}, u32[]{:S(2)}) collective-permute-start(bf16[1,2,256,2048]{2,3,1,0:T(8,128)(2,1)S(1)} %collective-permute-done.2), channel_id=1, source_target_pairs={{0,4},{4,8},{8,12},{12,16},{16,20},{20,24},{24,28},{28,0},{1,5},{5... | collective-permute-start | bytes 6291464 | tf_op jit(solution)/shard_map/ppermute | solution.py:14
  153.0 56.3 %collective-permute-start.5 = (bf16[1,2,256,2048]{2,3,1,0:T(8,128)(2,1)}, bf16[1,2,256,2048]{2,3,1,0:T(8,128)(2,1)}, u32[]{:S(2)}, u32[]{:S(2)}) collective-permute-start(bf16[1,2,256,2048]{2,3,1,0:T(8,128)(2,1)} %collective-permute-done.3), channel_id=1, source_target_pairs={{0,28},{4,0},{8,4},{12,8},{16,12},{20,16},{24,20},{28,24},{1,29},{... | collective-permute-start | bytes 6291464 | tf_op jit(solution)/shard_map/ppermute | solution.py:17
  199.7 26.7 %collective-permute-start.6 = (bf16[1,2,256,2048]{2,3,1,0:T(8,128)(2,1)}, bf16[1,2,256,2048]{2,3,1,0:T(8,128)(2,1)}, u32[]{:S(2)}, u32[]{:S(2)}) collective-permute-start(bf16[1,2,256,2048]{2,3,1,0:T(8,128)(2,1)} %collective-permute-done.4), channel_id=1, source_target_pairs={{0,4},{4,8},{8,12},{12,16},{16,20},{20,24},{24,28},{28,0},{1,5},{5... | collective-permute-start | bytes 6291464 | tf_op jit(solution)/shard_map/ppermute | solution.py:14
  201.7 1.6 copy-start.1
  201.7 2.2 copy-start.3
  203.3 1.7 copy-start.5
